TPU v7x, 512 devices: a whole 4x8x8 slice. The times are simulated.
512 devices in a mesh: rows: 64 (over y, x, core), dates: 8 (over z).
Axes of the slice: x: 4, y: 8, z: 8, core: 2. Of those that a mesh axis runs over, the one named last changes fastest.
Arguments:
- obs_mask: int32 [16, 512, 4096], P('dates', 'rows'), may hold values 0 or 1
- precision: float32 [16, 512, 4096], P('dates', 'rows'), may hold values from 0.5 to 4
- observed: float32 [16, 512, 4096], P('dates', 'rows')
- edge_class: int32 [2, 512, 4096], P(None, 'rows'), may hold values from 0 to 7
- temporal_weight: float32 [15], replicated, may hold values from 0.5 to 4
- inverse: bfloat16 [16, 16, 512, 4096], P(None, None, 'rows', 'dates'), as said below
Outputs:
- solution: float32 [16, 512, 4096], P('dates', 'rows')
- residual: float32 [16, 512, 4096], P('dates', 'rows')
Inputs may be any that keep to these rules, and one draw needn't show every extreme that they name: `inverse`: each pixel's matrix is symmetric with a diagonal larger than the sum of magnitudes of its row's other entries.
All inputs are finite; a program needn't handle non-finite values. No bound on the sum of `obs_mask` on one device may be relied on, other than what follows from the above.
Results may differ from a plain program's by a relative error of at most 0.0065.
Values sent between devices are 32-bit elements; how exact they have to be, the bound alone decides.
A program may use at most 64 MiB of HBM per device.

v0:
```python
import jax
import jax.numpy as jnp
from jax import lax
from jax.sharding import PartitionSpec as P

mass_term = 0.1


def shifted(value, axis, steps):
    count = lax.axis_size(axis)
    first, last = (max(0, -steps), min(count, count - steps))
    return lax.ppermute(value, axis, [(i, i + steps) for i in range(first, last)])


def apply_inverse(inverse, values):
    total = inverse[:, 0].astype(jnp.float32) * values[0][None]
    for source in range(1, values.shape[0]):
        total = total + inverse[:, source].astype(jnp.float32) * values[source][None]
    return total


def body(obs_mask, precision, observed, edge_class, temporal_weight, inverse):
    dates_here, rows_here, columns = observed.shape
    cols_here = inverse.shape[3]
    line_start = lax.axis_index("rows") * rows_here
    lines_total = rows_here * lax.axis_size("rows")
    col_start = lax.axis_index("dates") * cols_here
    weight = obs_mask.astype(jnp.float32) * precision
    both = jnp.stack([weight, weight * observed])
    both = lax.all_to_all(both, "dates", split_axis=3, concat_axis=1, tiled=True)
    weight, rhs = (both[0], both[1])
    classes = 0.25 * (edge_class.astype(jnp.float32) + 1.0)
    col_ids = lax.broadcasted_iota(jnp.int32, (rows_here, columns), 1)
    row_ids = lax.broadcasted_iota(jnp.int32, (rows_here, cols_here), 0) + line_start
    across_all = jnp.where(col_ids == columns - 1, 0.0, classes[0])
    across_ext = jnp.pad(across_all, ((0, 0), (1, 0)))
    across_prev = lax.dynamic_slice_in_dim(across_ext, col_start, cols_here, 1)
    across = lax.dynamic_slice_in_dim(across_all, col_start, cols_here, 1)
    downward = lax.dynamic_slice_in_dim(classes[1], col_start, cols_here, 1)
    downward = jnp.where(row_ids == lines_total - 1, 0.0, downward)
    downward_prev = jnp.concatenate([shifted(downward[-1:], "rows", 1), downward[:-1]], axis=0)
    zero_one = jnp.zeros((1,), jnp.float32)
    tau_up = jnp.concatenate([temporal_weight, zero_one])[:, None, None]
    tau_down = jnp.concatenate([zero_one, temporal_weight])[:, None, None]
    centre = (
        mass_term
        + weight
        + (across + across_prev + downward + downward_prev)[None]
        + (tau_up + tau_down)
    )

    def operator(field):
        above = jnp.concatenate([shifted(field[:, -1:], "rows", 1), field[:, :-1]], axis=1)
        below = jnp.concatenate([field[:, 1:], shifted(field[:, :1], "rows", -1)], axis=1)
        left = jnp.concatenate([shifted(field[:, :, -1:], "dates", 1), field[:, :, :-1]], axis=2)
        right = jnp.concatenate([field[:, :, 1:], shifted(field[:, :, :1], "dates", -1)], axis=2)
        before = jnp.pad(field, ((1, 0), (0, 0), (0, 0)))[:-1]
        after = jnp.pad(field, ((0, 1), (0, 0), (0, 0)))[1:]
        return (
            centre * field
            - (across * right + across_prev * left)
            - (downward * below + downward_prev * above)
            - (tau_up * after + tau_down * before)
        )

    precond = apply_inverse(inverse, rhs)
    image = operator(precond)
    mapped = apply_inverse(inverse, image)
    mapped_image = operator(mapped)
    sums = jnp.stack(
        [
            jnp.sum(rhs * precond),
            jnp.sum(precond * image),
            jnp.sum(image * mapped),
            jnp.sum(mapped * mapped_image),
        ]
    )
    sums = lax.psum(sums, ("rows", "dates"))
    rz, dd, ee, ff = (sums[0], sums[1], sums[2], sums[3])
    alpha = rz / dd
    grown = alpha * ee / dd
    alpha_next = (alpha * alpha * ee - rz) / (alpha * alpha * (ff - ee * ee / dd))
    first = alpha + alpha_next * grown
    second = alpha_next * alpha
    out = jnp.stack(
        [first * precond - second * mapped, rhs - first * image + second * mapped_image]
    )
    out = lax.all_to_all(out, "dates", split_axis=1, concat_axis=3, tiled=True)
    return (out[0], out[1])


def solution(mesh):
    return jax.shard_map(
        body,
        mesh=mesh,
        in_specs=(
            P("dates", "rows", None),
            P("dates", "rows", None),
            P("dates", "rows", None),
            P(None, "rows", None),
            P(),
            P(None, None, "rows", "dates"),
        ),
        out_specs=(P("dates", "rows", None), P("dates", "rows", None)),
        check_vma=False,
    )
```

profile of v0, /device:TPU:26, one launch (start us, length us, event | category | flops | bytes accessed | tf_op | source)
XLA Modules:
  0.0 248.5 jit_solution(16082085440796772396)
XLA Ops:
  1.8 8.2 %copy.156 = f32[2,2,8,4096]{2,1,0,3:T(2,128)} copy(f32[2,2,8,4096]{3,2,1,0:T(8,128)S(1)} %pad_maximum_fusion) | data formatting | bytes 1048576 | tf_op jit(solution)/shard_map/stack | solution.py:29
  10.0 15.6 %reshape.805 = f32[8,1,16384]{2,1,0:T(1,128)} reshape(f32[4096,2,2,8]{3,2,1,0:T(2,128)} %bitcast.617) | data formatting | bytes 1048576
  25.7 10.4 %all-to-all-start = ((f32[8,1,16384]{2,1,0:T(1,128)}), f32[8,1,16384]{2,1,0:T(1,128)S(1)}, u32[]{:S(2)}, u32[]{:S(2)}) async-start(f32[8,1,16384]{2,1,0:T(1,128)} %reshape.805), calls=%async_computation | async-start | bytes 1048576 | tf_op jit(solution)/shard_map/all_to_all | solution.py:30
  36.3 2.1 collective-permute-start
  39.1 1.9 bitcast_convert_fusion.15
  42.4 11.2 %all-to-all-done = f32[8,1,16384]{2,1,0:T(1,128)S(1)} async-done(((f32[8,1,16384]{2,1,0:T(1,128)}), f32[8,1,16384]{2,1,0:T(1,128)S(1)}, u32[]{:S(2)}, u32[]{:S(2)}) %all-to-all-start) | async-done | bytes 524320 | tf_op jit(solution)/shard_map/all_to_all | solution.py:30
  54.1 1.9 reduce.1
  56.0 16.0 %reshape.806 = f32[4096,2,2,8]{3,2,1,0:T(2,128)} reshape(f32[8,16384]{1,0:T(8,128)S(1)} %reduce.1) | data formatting | bytes 1048576
  72.0 10.1 %copy.158 = f32[2,2,8,8,512]{4,2,1,3,0:T(8,128)S(1)} copy(f32[2,2,8,8,512]{2,1,0,4,3:T(2,128)} %bitcast.618) | data formatting | bytes 1048576 | tf_op jit(solution)/shard_map/all_to_all | solution.py:30
  83.1 1.4 collective-permute-start.1
  84.5 4.5 %collective-permute-start.2 = (f32[16,8,1]{2,1,0:T(8,128)S(1)}, f32[16,8,1]{2,1,0:T(8,128)S(1)}, u32[]{:S(2)}, u32[]{:S(2)}) collective-permute-start(f32[16,8,1]{2,1,0:T(8,128)S(1)} %get-tuple-element.60), channel_id=1, source_target_pairs={{0,1},{1,2},{2,3},{3,4},{4,5},{5,6},{6,7},{8,9},{9,10},{10,11},{11... | collective-permute-start | bytes 1544 | tf_op jit(solution)/shard_map/ppermute | solution.py:12
  89.1 1.9 collective-permute-start.3
  91.0 2.4 collective-permute-start.4
  93.6 1.2 multiply_reduce_fusion.3
  97.3 1.3 collective-permute-start.5
  98.6 4.5 %collective-permute-start.6 = (f32[16,8,1]{2,1,0:T(8,128)S(1)}, f32[16,8,1]{2,1,0:T(8,128)S(1)}, u32[]{:S(2)}, u32[]{:S(2)}) collective-permute-start(f32[16,8,1]{2,1,0:T(8,128)S(1)} %get-tuple-element.35), channel_id=1, source_target_pairs={{0,1},{1,2},{2,3},{3,4},{4,5},{5,6},{6,7},{8,9},{9,10},{10,11},{11... | collective-permute-start | bytes 1544 | tf_op jit(solution)/shard_map/ppermute | solution.py:12
  103.2 1.9 collective-permute-start.7
  105.1 2.6 %collective-permute-start.8 = (f32[16,1,512]{2,1,0:T(1,128)S(1)}, f32[16,1,512]{2,1,0:T(1,128)S(1)}, u32[]{:S(2)}, u32[]{:S(2)}) collective-permute-start(f32[16,1,512]{2,1,0:T(1,128)S(1)} %get-tuple-element.39), channel_id=1, source_target_pairs={{0,8},{8,16},{16,24},{24,32},{32,40},{40,48},{48,56},{56,64},{64,7... | collective-permute-start | bytes 98312 | tf_op jit(solution)/shard_map/ppermute | solution.py:12
  107.8 5.2 %collective-permute-done.8 = f32[16,1,512]{2,1,0:T(1,128)S(1)} collective-permute-done((f32[16,1,512]{2,1,0:T(1,128)S(1)}, f32[16,1,512]{2,1,0:T(1,128)S(1)}, u32[]{:S(2)}, u32[]{:S(2)}) %collective-permute-start.8) | collective-permute-done | bytes 32800 | tf_op jit(solution)/shard_map/ppermute | solution.py:12
  113.1 1.5 multiply_reduce_fusion.2
  114.6 2.6 %pad_maximum_fusion.5 = f32[4]{0:T(128)S(1)} fusion(f32[1]{0:T(128)} %bitcast.76, f32[1]{0:T(128)} %bitcast.75, f32[1]{0:T(128)} %bitcast.58, f32[1]{0:T(128)} %bitcast.37), kind=kLoop, calls=%fused_computation.229 | loop fusion | flops 12 | bytes 32 | tf_op jit(solution)/shard_map/stack | solution.py:70
  117.2 100.8 %psum.7 = f32[4]{0:T(128)S(1)} all-reduce(f32[4]{0:T(128)S(1)} %pad_maximum_fusion.5), channel_id=1, replica_groups=mesh['rows'=64,'dates'=8] {'rows','dates'}, use_global_device_ids=true, to_apply=%region_4.5 | all-reduce | flops 4 | bytes 32 | tf_op jit(solution)/shard_map/psum | solution.py:78
  225.1 1.6 fusion.19
  226.8 20.2 %all_to_all.30 = f32[2,16,8,512]{3,2,0,1:T(8,128)S(1)} all-to-all(f32[2,16,8,512]{3,2,0,1:T(8,128)S(1)} %pad_maximum_fusion.1), channel_id=1, replica_groups=mesh['rows'=64,'dates'=8] {'dates'}, dimensions={1} | all-to-all | bytes 1048576 | tf_op jit(solution)/shard_map/all_to_all | solution.py:88
  (107 shorter events, 9.3 us)
Async XLA Ops:
  10.0 26.1 %copy-start.23 = (s32[2,8,4096]{2,1,0:T(8,128)S(1)}, s32[2,8,4096]{2,1,0:T(8,128)}, u32[]{:S(2)}) copy-start(s32[2,8,4096]{2,1,0:T(8,128)} %param.9) | copy-start | bytes 786436
  25.7 13.4 %copy-start = (bf16[16,16,8,512]{3,2,1,0:T(8,128)(2,1)S(1)}, bf16[16,16,8,512]{3,2,1,0:T(8,128)(2,1)}, u32[]{:S(2)}) copy-start(bf16[16,16,8,512]{3,2,1,0:T(8,128)(2,1)} %param.11) | copy-start | bytes 6291460
  25.7 27.9 %all-to-all-start = ((f32[8,1,16384]{2,1,0:T(1,128)}), f32[8,1,16384]{2,1,0:T(1,128)S(1)}, u32[]{:S(2)}, u32[]{:S(2)}) async-start(f32[8,1,16384]{2,1,0:T(1,128)} %reshape.805), calls=%async_computation | async-start | bytes 1048576 | tf_op jit(solution)/shard_map/all_to_all | solution.py:30
  36.3 5.4 %collective-permute-start = (f32[1,512]{1,0:T(1,128)S(1)}, f32[1,512]{1,0:T(1,128)S(1)}, u32[]{:S(2)}, u32[]{:S(2)}) collective-permute-start(f32[1,512]{1,0:T(1,128)S(1)} %slice.360), channel_id=1, source_target_pairs={{0,8},{8,16},{16,24},{24,32},{32,40},{40,48},{48,56},{56,64},{64,7... | collective-permute-start | bytes 6152 | tf_op jit(solution)/shard_map/ppermute | solution.py:12
  82.2 30.8 %copy-start.16 = (f32[8,512]{1,0:T(8,128)}, f32[8,512]{1,0:T(8,128)S(1)}, u32[]{:S(2)}) copy-start(f32[8,512]{1,0:T(8,128)S(1)} %get-tuple-element.73) | copy-start | bytes 49156
  82.2 30.8 %copy-start.17 = (f32[8,512]{1,0:T(8,128)}, f32[8,512]{1,0:T(8,128)S(1)}, u32[]{:S(2)}) copy-start(f32[8,512]{1,0:T(8,128)S(1)} %get-tuple-element.74) | copy-start | bytes 49156
  82.2 30.8 %copy-start.18 = (f32[8,512]{1,0:T(8,128)}, f32[8,512]{1,0:T(8,128)S(1)}, u32[]{:S(2)}) copy-start(f32[8,512]{1,0:T(8,128)S(1)} %get-tuple-element.75) | copy-start | bytes 49156
  82.3 30.8 %copy-start.19 = (f32[8,512]{1,0:T(8,128)}, f32[8,512]{1,0:T(8,128)S(1)}, u32[]{:S(2)}) copy-start(f32[8,512]{1,0:T(8,128)S(1)} %get-tuple-element.76) | copy-start | bytes 49156
  82.3 30.8 %copy-start.20 = (f32[8,512]{1,0:T(8,128)}, f32[8,512]{1,0:T(8,128)S(1)}, u32[]{:S(2)}) copy-start(f32[8,512]{1,0:T(8,128)S(1)} %get-tuple-element.77) | copy-start | bytes 49156
  82.3 30.8 %copy-start.21 = (f32[8,512]{1,0:T(8,128)}, f32[8,512]{1,0:T(8,128)S(1)}, u32[]{:S(2)}) copy-start(f32[8,512]{1,0:T(8,128)S(1)} %get-tuple-element.78) | copy-start | bytes 49156
  82.3 30.8 %copy-start.22 = (f32[8,512]{1,0:T(8,128)}, f32[8,512]{1,0:T(8,128)S(1)}, u32[]{:S(2)}) copy-start(f32[8,512]{1,0:T(8,128)S(1)} %get-tuple-element.79) | copy-start | bytes 49156
  82.3 11.1 %copy-start.1 = (f32[16,1,8,512]{3,2,0,1:T(8,128)S(1)}, f32[16,1,8,512]{3,2,0,1:T(8,128)}, u32[]{:S(2)}) copy-start(f32[16,1,8,512]{3,2,0,1:T(8,128)} %get-tuple-element.11) | copy-start | bytes 786436
  82.3 11.1 %copy-start.2 = (f32[16,1,8,512]{3,2,0,1:T(8,128)S(1)}, f32[16,1,8,512]{3,2,0,1:T(8,128)}, u32[]{:S(2)}) copy-start(f32[16,1,8,512]{3,2,0,1:T(8,128)} %get-tuple-element.12) | copy-start | bytes 786436
  82.3 11.1 %copy-start.3 = (f32[16,1,8,512]{3,2,0,1:T(8,128)S(1)}, f32[16,1,8,512]{3,2,0,1:T(8,128)}, u32[]{:S(2)}) copy-start(f32[16,1,8,512]{3,2,0,1:T(8,128)} %get-tuple-element.13) | copy-start | bytes 786436
  82.3 11.1 %copy-start.4 = (f32[16,1,8,512]{3,2,0,1:T(8,128)S(1)}, f32[16,1,8,512]{3,2,0,1:T(8,128)}, u32[]{:S(2)}) copy-start(f32[16,1,8,512]{3,2,0,1:T(8,128)} %get-tuple-element.14) | copy-start | bytes 786436
  82.3 11.1 %copy-start.5 = (f32[16,1,8,512]{3,2,0,1:T(8,128)S(1)}, f32[16,1,8,512]{3,2,0,1:T(8,128)}, u32[]{:S(2)}) copy-start(f32[16,1,8,512]{3,2,0,1:T(8,128)} %get-tuple-element.15) | copy-start | bytes 786436
  83.1 11.9 %collective-permute-start.1 = (f32[16,8,1]{2,1,0:T(8,128)S(1)}, f32[16,8,1]{2,1,0:T(8,128)S(1)}, u32[]{:S(2)}, u32[]{:S(2)}) collective-permute-start(f32[16,8,1]{2,1,0:T(8,128)S(1)} %get-tuple-element.61), channel_id=1, source_target_pairs={{1,0},{2,1},{3,2},{4,3},{5,4},{6,5},{7,6},{9,8},{10,9},{11,10},{12... | collective-permute-start | bytes 1544 | tf_op jit(solution)/shard_map/ppermute | solution.py:12
  84.5 10.5 %collective-permute-start.2 = (f32[16,8,1]{2,1,0:T(8,128)S(1)}, f32[16,8,1]{2,1,0:T(8,128)S(1)}, u32[]{:S(2)}, u32[]{:S(2)}) collective-permute-start(f32[16,8,1]{2,1,0:T(8,128)S(1)} %get-tuple-element.60), channel_id=1, source_target_pairs={{0,1},{1,2},{2,3},{3,4},{4,5},{5,6},{6,7},{8,9},{9,10},{10,11},{11... | collective-permute-start | bytes 1544 | tf_op jit(solution)/shard_map/ppermute | solution.py:12
  89.1 6.0 %collective-permute-start.3 = (f32[16,1,512]{2,1,0:T(1,128)S(1)}, f32[16,1,512]{2,1,0:T(1,128)S(1)}, u32[]{:S(2)}, u32[]{:S(2)}) collective-permute-start(f32[16,1,512]{2,1,0:T(1,128)S(1)} %get-tuple-element.57), channel_id=1, source_target_pairs={{8,0},{16,8},{24,16},{32,24},{40,32},{48,40},{56,48},{64,56},{72,6... | collective-permute-start | bytes 98312 | tf_op jit(solution)/shard_map/ppermute | solution.py:12
  91.0 5.2 %collective-permute-start.4 = (f32[16,1,512]{2,1,0:T(1,128)S(1)}, f32[16,1,512]{2,1,0:T(1,128)S(1)}, u32[]{:S(2)}, u32[]{:S(2)}) collective-permute-start(f32[16,1,512]{2,1,0:T(1,128)S(1)} %get-tuple-element.56), channel_id=1, source_target_pairs={{0,8},{8,16},{16,24},{24,32},{32,40},{40,48},{48,56},{56,64},{64,7... | collective-permute-start | bytes 98312 | tf_op jit(solution)/shard_map/ppermute | solution.py:12
  97.3 10.5 %collective-permute-start.5 = (f32[16,8,1]{2,1,0:T(8,128)S(1)}, f32[16,8,1]{2,1,0:T(8,128)S(1)}, u32[]{:S(2)}, u32[]{:S(2)}) collective-permute-start(f32[16,8,1]{2,1,0:T(8,128)S(1)} %get-tuple-element.34), channel_id=1, source_target_pairs={{1,0},{2,1},{3,2},{4,3},{5,4},{6,5},{7,6},{9,8},{10,9},{11,10},{12... | collective-permute-start | bytes 1544 | tf_op jit(solution)/shard_map/ppermute | solution.py:12
  98.6 9.2 %collective-permute-start.6 = (f32[16,8,1]{2,1,0:T(8,128)S(1)}, f32[16,8,1]{2,1,0:T(8,128)S(1)}, u32[]{:S(2)}, u32[]{:S(2)}) collective-permute-start(f32[16,8,1]{2,1,0:T(8,128)S(1)} %get-tuple-element.35), channel_id=1, source_target_pairs={{0,1},{1,2},{2,3},{3,4},{4,5},{5,6},{6,7},{8,9},{9,10},{10,11},{11... | collective-permute-start | bytes 1544 | tf_op jit(solution)/shard_map/ppermute | solution.py:12
  103.2 4.6 %collective-permute-start.7 = (f32[16,1,512]{2,1,0:T(1,128)S(1)}, f32[16,1,512]{2,1,0:T(1,128)S(1)}, u32[]{:S(2)}, u32[]{:S(2)}) collective-permute-start(f32[16,1,512]{2,1,0:T(1,128)S(1)} %get-tuple-element.38), channel_id=1, source_target_pairs={{8,0},{16,8},{24,16},{32,24},{40,32},{48,40},{56,48},{64,56},{72,6... | collective-permute-start | bytes 98312 | tf_op jit(solution)/shard_map/ppermute | solution.py:12
  105.1 7.9 %collective-permute-start.8 = (f32[16,1,512]{2,1,0:T(1,128)S(1)}, f32[16,1,512]{2,1,0:T(1,128)S(1)}, u32[]{:S(2)}, u32[]{:S(2)}) collective-permute-start(f32[16,1,512]{2,1,0:T(1,128)S(1)} %get-tuple-element.39), channel_id=1, source_target_pairs={{0,8},{8,16},{16,24},{24,32},{32,40},{40,48},{48,56},{56,64},{64,7... | collective-permute-start | bytes 98312 | tf_op jit(solution)/shard_map/ppermute | solution.py:12
  (19 other events, 134.2 us)
where the time goes:
time: 249 us; the launch traced here: 248 us
  blocking collectives  121 us (49%)
  local copies, waits for them, and re-layouts  53.4 us (21%)
  starting transfers between devices  33.2 us (13%)
  waiting for transfers between devices  17.6 us (7%)
  other arithmetic  15.4 us (6%)
  between operations  7.91 us (3%)
    psum x1, blocking collectives, body(): sums = lax.psum(sums, ('rows', 'dates'))  101 us
    unnamed x68, local copies, waits for them, and re-layouts  31.8 us
    ppermute x9, starting transfers between devices, shifted(): lax.ppermute(value, axis, [(i, i + steps) for i in range(first, last)])  22.8 us
    all_to_all x1, blocking collectives, body(): out = lax.all_to_all(out, 'dates', split_axis=1, concat_axis=3, tiled=True)  20.2 us
    all_to_all x1, waiting for transfers between devices, body(): lax.all_to_all(both, 'dates', split_axis=3, concat_axis=1, tiled=True)  11.2 us
    all_to_all x2, local copies, waits for them, and re-layouts, body(): lax.all_to_all(both, 'dates', split_axis=3, concat_axis=1, tiled=True)  10.6 us
    all_to_all x1, starting transfers between devices, body(): lax.all_to_all(both, 'dates', split_axis=3, concat_axis=1, tiled=True)  10.4 us
    another operation x1, local copies, waits for them, and re-layouts, body(): both = jnp.stack([weight, weight * observed])  8.2 us
  transfers between devices with their start and end apart: 10, of which 3 were waited for; matrix products, arithmetic and copies ran while one was open for 2% of the time, Pallas kernels for 0%

commit v1 on v0

--- a/solution.py
+++ b/solution.py
@@ -75,7 +75,7 @@
             jnp.sum(mapped * mapped_image),
         ]
     )
-    sums = lax.psum(sums, ("rows", "dates"))
+    sums = lax.psum(lax.psum(sums, "dates"), "rows")
     rz, dd, ee, ff = (sums[0], sums[1], sums[2], sums[3])
     alpha = rz / dd
     grown = alpha * ee / dd

time: 249 us -> 294 us (1.18)
  the two profiles are of different devices: /device:TPU:26 before, /device:TPU:32 now
where the time goes in v1:
time: 294 us; the launch traced here: 293 us
  blocking collectives  160 us (54%)
  local copies, waits for them, and re-layouts  53.4 us (18%)
  starting transfers between devices  34.4 us (12%)
  waiting for transfers between devices  22.1 us (8%)
  other arithmetic  15.2 us (5%)
  between operations  7.68 us (3%)
    psum x2, blocking collectives, body(): sums = lax.psum(lax.psum(sums, 'dates'), 'rows')  138 us
    unnamed x68, local copies, waits for them, and re-layouts  31.8 us
    ppermute x9, starting transfers between devices, shifted(): lax.ppermute(value, axis, [(i, i + steps) for i in range(first, last)])  24 us
    all_to_all x1, blocking collectives, body(): out = lax.all_to_all(out, 'dates', split_axis=1, concat_axis=3, tiled=True)  21.6 us
    ppermute x9, waiting for transfers between devices, shifted(): lax.ppermute(value, axis, [(i, i + steps) for i in range(first, last)])  13.7 us
    all_to_all x2, local copies, waits for them, and re-layouts, body(): lax.all_to_all(both, 'dates', split_axis=3, concat_axis=1, tiled=True)  10.6 us
    all_to_all x1, starting transfers between devices, body(): lax.all_to_all(both, 'dates', split_axis=3, concat_axis=1, tiled=True)  10.4 us
    all_to_all x1, waiting for transfers between devices, body(): lax.all_to_all(both, 'dates', split_axis=3, concat_axis=1, tiled=True)  8.42 us
  transfers between devices with their start and end apart: 10, of which 4 were waited for; matrix products, arithmetic and copies ran while one was open for 2% of the time, Pallas kernels for 0%

profile of v1, /device:TPU:32, one launch (start us, length us, event | category | flops | bytes accessed | tf_op | source)
XLA Modules:
  0.0 292.9 jit_solution(13214234882895071796)
XLA Ops:
  1.8 8.2 %copy.156 = f32[2,2,8,4096]{2,1,0,3:T(2,128)} copy(f32[2,2,8,4096]{3,2,1,0:T(8,128)S(1)} %pad_maximum_fusion) | data formatting | bytes 1048576 | tf_op jit(solution)/shard_map/stack | solution.py:29
  10.0 15.6 %reshape.805 = f32[8,1,16384]{2,1,0:T(1,128)} reshape(f32[4096,2,2,8]{3,2,1,0:T(2,128)} %bitcast.617) | data formatting | bytes 1048576
  25.7 10.4 %all-to-all-start = ((f32[8,1,16384]{2,1,0:T(1,128)}), f32[8,1,16384]{2,1,0:T(1,128)S(1)}, u32[]{:S(2)}, u32[]{:S(2)}) async-start(f32[8,1,16384]{2,1,0:T(1,128)} %reshape.805), calls=%async_computation | async-start | bytes 1048576 | tf_op jit(solution)/shard_map/all_to_all | solution.py:30
  36.3 2.1 collective-permute-start
  39.1 1.9 bitcast_convert_fusion.15
  41.7 2.8 collective-permute-done
  45.2 8.4 %all-to-all-done = f32[8,1,16384]{2,1,0:T(1,128)S(1)} async-done(((f32[8,1,16384]{2,1,0:T(1,128)}), f32[8,1,16384]{2,1,0:T(1,128)S(1)}, u32[]{:S(2)}, u32[]{:S(2)}) %all-to-all-start) | async-done | bytes 524320 | tf_op jit(solution)/shard_map/all_to_all | solution.py:30
  54.1 1.9 reduce.1
  56.0 16.0 %reshape.806 = f32[4096,2,2,8]{3,2,1,0:T(2,128)} reshape(f32[8,16384]{1,0:T(8,128)S(1)} %reduce.1) | data formatting | bytes 1048576
  72.1 10.1 %copy.158 = f32[2,2,8,8,512]{4,2,1,3,0:T(8,128)S(1)} copy(f32[2,2,8,8,512]{2,1,0,4,3:T(2,128)} %bitcast.618) | data formatting | bytes 1048576 | tf_op jit(solution)/shard_map/all_to_all | solution.py:30
  84.5 4.5 %collective-permute-start.2 = (f32[16,8,1]{2,1,0:T(8,128)S(1)}, f32[16,8,1]{2,1,0:T(8,128)S(1)}, u32[]{:S(2)}, u32[]{:S(2)}) collective-permute-start(f32[16,8,1]{2,1,0:T(8,128)S(1)} %get-tuple-element.60), channel_id=1, source_target_pairs={{0,1},{1,2},{2,3},{3,4},{4,5},{5,6},{6,7},{8,9},{9,10},{10,11},{11... | collective-permute-start | bytes 1544 | tf_op jit(solution)/shard_map/ppermute | solution.py:12
  89.1 3.6 %collective-permute-start.3 = (f32[16,1,512]{2,1,0:T(1,128)S(1)}, f32[16,1,512]{2,1,0:T(1,128)S(1)}, u32[]{:S(2)}, u32[]{:S(2)}) collective-permute-start(f32[16,1,512]{2,1,0:T(1,128)S(1)} %get-tuple-element.57), channel_id=1, source_target_pairs={{8,0},{16,8},{24,16},{32,24},{40,32},{48,40},{56,48},{64,56},{72,6... | collective-permute-start | bytes 98312 | tf_op jit(solution)/shard_map/ppermute | solution.py:12
  92.7 1.9 collective-permute-start.4
  96.2 5.1 %collective-permute-done.4 = f32[16,1,512]{2,1,0:T(1,128)S(1)} collective-permute-done((f32[16,1,512]{2,1,0:T(1,128)S(1)}, f32[16,1,512]{2,1,0:T(1,128)S(1)}, u32[]{:S(2)}, u32[]{:S(2)}) %collective-permute-start.4) | collective-permute-done | bytes 32800 | tf_op jit(solution)/shard_map/ppermute | solution.py:12
  103.7 4.5 %collective-permute-start.6 = (f32[16,8,1]{2,1,0:T(8,128)S(1)}, f32[16,8,1]{2,1,0:T(8,128)S(1)}, u32[]{:S(2)}, u32[]{:S(2)}) collective-permute-start(f32[16,8,1]{2,1,0:T(8,128)S(1)} %get-tuple-element.35), channel_id=1, source_target_pairs={{0,1},{1,2},{2,3},{3,4},{4,5},{5,6},{6,7},{8,9},{9,10},{10,11},{11... | collective-permute-start | bytes 1544 | tf_op jit(solution)/shard_map/ppermute | solution.py:12
  108.2 1.9 collective-permute-start.7
  110.2 2.6 collective-permute-start.8
  112.9 5.8 %collective-permute-done.8 = f32[16,1,512]{2,1,0:T(1,128)S(1)} collective-permute-done((f32[16,1,512]{2,1,0:T(1,128)S(1)}, f32[16,1,512]{2,1,0:T(1,128)S(1)}, u32[]{:S(2)}, u32[]{:S(2)}) %collective-permute-start.8) | collective-permute-done | bytes 32800 | tf_op jit(solution)/shard_map/ppermute | solution.py:12
  118.8 1.5 multiply_reduce_fusion.2
  120.2 2.6 pad_maximum_fusion.5
  122.8 14.4 %psum.14 = f32[4]{0:T(128)S(1)} all-reduce(f32[4]{0:T(128)S(1)} %pad_maximum_fusion.5), channel_id=1, replica_groups=mesh['rows'=64,'dates'=8] {'dates'}, use_global_device_ids=true, to_apply=%region_4.5 | all-reduce | flops 4 | bytes 32 | tf_op jit(solution)/shard_map/psum | solution.py:78
  137.2 124.0 %psum.15 = f32[4]{0:T(128)S(1)} all-reduce(f32[4]{0:T(128)S(1)} %psum.14), channel_id=1, replica_groups=mesh['rows'=64,'dates'=8] {'rows'}, use_global_device_ids=true, to_apply=%region_5.6 | all-reduce | flops 4 | bytes 32 | tf_op jit(solution)/shard_map/psum | solution.py:78
  268.2 1.6 fusion.19
  269.9 21.6 %all_to_all.30 = f32[2,16,8,512]{3,2,0,1:T(8,128)S(1)} all-to-all(f32[2,16,8,512]{3,2,0,1:T(8,128)S(1)} %pad_maximum_fusion.1), channel_id=1, replica_groups=mesh['rows'=64,'dates'=8] {'dates'}, dimensions={1} | all-to-all | bytes 1048576 | tf_op jit(solution)/shard_map/all_to_all | solution.py:88
  (108 shorter events, 12.0 us)
Async XLA Ops:
  10.0 26.1 %copy-start.23 = (s32[2,8,4096]{2,1,0:T(8,128)S(1)}, s32[2,8,4096]{2,1,0:T(8,128)}, u32[]{:S(2)}) copy-start(s32[2,8,4096]{2,1,0:T(8,128)} %param.9) | copy-start | bytes 786436
  25.7 13.4 %copy-start = (bf16[16,16,8,512]{3,2,1,0:T(8,128)(2,1)S(1)}, bf16[16,16,8,512]{3,2,1,0:T(8,128)(2,1)}, u32[]{:S(2)}) copy-start(bf16[16,16,8,512]{3,2,1,0:T(8,128)(2,1)} %param.11) | copy-start | bytes 6291460
  25.7 27.9 %all-to-all-start = ((f32[8,1,16384]{2,1,0:T(1,128)}), f32[8,1,16384]{2,1,0:T(1,128)S(1)}, u32[]{:S(2)}, u32[]{:S(2)}) async-start(f32[8,1,16384]{2,1,0:T(1,128)} %reshape.805), calls=%async_computation | async-start | bytes 1048576 | tf_op jit(solution)/shard_map/all_to_all | solution.py:30
  36.3 8.2 %collective-permute-start = (f32[1,512]{1,0:T(1,128)S(1)}, f32[1,512]{1,0:T(1,128)S(1)}, u32[]{:S(2)}, u32[]{:S(2)}) collective-permute-start(f32[1,512]{1,0:T(1,128)S(1)} %slice.360), channel_id=1, source_target_pairs={{0,8},{8,16},{16,24},{24,32},{32,40},{40,48},{48,56},{56,64},{64,7... | collective-permute-start | bytes 6152 | tf_op jit(solution)/shard_map/ppermute | solution.py:12
  82.3 36.5 %copy-start.16 = (f32[8,512]{1,0:T(8,128)}, f32[8,512]{1,0:T(8,128)S(1)}, u32[]{:S(2)}) copy-start(f32[8,512]{1,0:T(8,128)S(1)} %get-tuple-element.73) | copy-start | bytes 49156
  82.3 36.4 %copy-start.17 = (f32[8,512]{1,0:T(8,128)}, f32[8,512]{1,0:T(8,128)S(1)}, u32[]{:S(2)}) copy-start(f32[8,512]{1,0:T(8,128)S(1)} %get-tuple-element.74) | copy-start | bytes 49156
  82.3 36.4 %copy-start.18 = (f32[8,512]{1,0:T(8,128)}, f32[8,512]{1,0:T(8,128)S(1)}, u32[]{:S(2)}) copy-start(f32[8,512]{1,0:T(8,128)S(1)} %get-tuple-element.75) | copy-start | bytes 49156
  82.3 36.4 %copy-start.19 = (f32[8,512]{1,0:T(8,128)}, f32[8,512]{1,0:T(8,128)S(1)}, u32[]{:S(2)}) copy-start(f32[8,512]{1,0:T(8,128)S(1)} %get-tuple-element.76) | copy-start | bytes 49156
  82.3 36.4 %copy-start.20 = (f32[8,512]{1,0:T(8,128)}, f32[8,512]{1,0:T(8,128)S(1)}, u32[]{:S(2)}) copy-start(f32[8,512]{1,0:T(8,128)S(1)} %get-tuple-element.77) | copy-start | bytes 49156
  82.3 36.4 %copy-start.21 = (f32[8,512]{1,0:T(8,128)}, f32[8,512]{1,0:T(8,128)S(1)}, u32[]{:S(2)}) copy-start(f32[8,512]{1,0:T(8,128)S(1)} %get-tuple-element.78) | copy-start | bytes 49156
  82.3 36.4 %copy-start.22 = (f32[8,512]{1,0:T(8,128)}, f32[8,512]{1,0:T(8,128)S(1)}, u32[]{:S(2)}) copy-start(f32[8,512]{1,0:T(8,128)S(1)} %get-tuple-element.79) | copy-start | bytes 49156
  82.3 12.3 %copy-start.1 = (f32[16,1,8,512]{3,2,0,1:T(8,128)S(1)}, f32[16,1,8,512]{3,2,0,1:T(8,128)}, u32[]{:S(2)}) copy-start(f32[16,1,8,512]{3,2,0,1:T(8,128)} %get-tuple-element.11) | copy-start | bytes 786436
  82.4 12.3 %copy-start.2 = (f32[16,1,8,512]{3,2,0,1:T(8,128)S(1)}, f32[16,1,8,512]{3,2,0,1:T(8,128)}, u32[]{:S(2)}) copy-start(f32[16,1,8,512]{3,2,0,1:T(8,128)} %get-tuple-element.12) | copy-start | bytes 786436
  82.4 12.3 %copy-start.3 = (f32[16,1,8,512]{3,2,0,1:T(8,128)S(1)}, f32[16,1,8,512]{3,2,0,1:T(8,128)}, u32[]{:S(2)}) copy-start(f32[16,1,8,512]{3,2,0,1:T(8,128)} %get-tuple-element.13) | copy-start | bytes 786436
  82.4 12.3 %copy-start.4 = (f32[16,1,8,512]{3,2,0,1:T(8,128)S(1)}, f32[16,1,8,512]{3,2,0,1:T(8,128)}, u32[]{:S(2)}) copy-start(f32[16,1,8,512]{3,2,0,1:T(8,128)} %get-tuple-element.14) | copy-start | bytes 786436
  82.4 12.3 %copy-start.5 = (f32[16,1,8,512]{3,2,0,1:T(8,128)S(1)}, f32[16,1,8,512]{3,2,0,1:T(8,128)}, u32[]{:S(2)}) copy-start(f32[16,1,8,512]{3,2,0,1:T(8,128)} %get-tuple-element.15) | copy-start | bytes 786436
  83.1 13.1 %collective-permute-start.1 = (f32[16,8,1]{2,1,0:T(8,128)S(1)}, f32[16,8,1]{2,1,0:T(8,128)S(1)}, u32[]{:S(2)}, u32[]{:S(2)}) collective-permute-start(f32[16,8,1]{2,1,0:T(8,128)S(1)} %get-tuple-element.61), channel_id=1, source_target_pairs={{1,0},{2,1},{3,2},{4,3},{5,4},{6,5},{7,6},{9,8},{10,9},{11,10},{12... | collective-permute-start | bytes 1544 | tf_op jit(solution)/shard_map/ppermute | solution.py:12
  84.5 11.7 %collective-permute-start.2 = (f32[16,8,1]{2,1,0:T(8,128)S(1)}, f32[16,8,1]{2,1,0:T(8,128)S(1)}, u32[]{:S(2)}, u32[]{:S(2)}) collective-permute-start(f32[16,8,1]{2,1,0:T(8,128)S(1)} %get-tuple-element.60), channel_id=1, source_target_pairs={{0,1},{1,2},{2,3},{3,4},{4,5},{5,6},{6,7},{8,9},{9,10},{10,11},{11... | collective-permute-start | bytes 1544 | tf_op jit(solution)/shard_map/ppermute | solution.py:12
  89.1 7.1 %collective-permute-start.3 = (f32[16,1,512]{2,1,0:T(1,128)S(1)}, f32[16,1,512]{2,1,0:T(1,128)S(1)}, u32[]{:S(2)}, u32[]{:S(2)}) collective-permute-start(f32[16,1,512]{2,1,0:T(1,128)S(1)} %get-tuple-element.57), channel_id=1, source_target_pairs={{8,0},{16,8},{24,16},{32,24},{40,32},{48,40},{56,48},{64,56},{72,6... | collective-permute-start | bytes 98312 | tf_op jit(solution)/shard_map/ppermute | solution.py:12
  92.7 8.6 %collective-permute-start.4 = (f32[16,1,512]{2,1,0:T(1,128)S(1)}, f32[16,1,512]{2,1,0:T(1,128)S(1)}, u32[]{:S(2)}, u32[]{:S(2)}) collective-permute-start(f32[16,1,512]{2,1,0:T(1,128)S(1)} %get-tuple-element.56), channel_id=1, source_target_pairs={{0,8},{8,16},{16,24},{24,32},{32,40},{40,48},{48,56},{56,64},{64,7... | collective-permute-start | bytes 98312 | tf_op jit(solution)/shard_map/ppermute | solution.py:12
  102.4 10.5 %collective-permute-start.5 = (f32[16,8,1]{2,1,0:T(8,128)S(1)}, f32[16,8,1]{2,1,0:T(8,128)S(1)}, u32[]{:S(2)}, u32[]{:S(2)}) collective-permute-start(f32[16,8,1]{2,1,0:T(8,128)S(1)} %get-tuple-element.34), channel_id=1, source_target_pairs={{1,0},{2,1},{3,2},{4,3},{5,4},{6,5},{7,6},{9,8},{10,9},{11,10},{12... | collective-permute-start | bytes 1544 | tf_op jit(solution)/shard_map/ppermute | solution.py:12
  103.7 9.2 %collective-permute-start.6 = (f32[16,8,1]{2,1,0:T(8,128)S(1)}, f32[16,8,1]{2,1,0:T(8,128)S(1)}, u32[]{:S(2)}, u32[]{:S(2)}) collective-permute-start(f32[16,8,1]{2,1,0:T(8,128)S(1)} %get-tuple-element.35), channel_id=1, source_target_pairs={{0,1},{1,2},{2,3},{3,4},{4,5},{5,6},{6,7},{8,9},{9,10},{10,11},{11... | collective-permute-start | bytes 1544 | tf_op jit(solution)/shard_map/ppermute | solution.py:12
  108.2 4.6 %collective-permute-start.7 = (f32[16,1,512]{2,1,0:T(1,128)S(1)}, f32[16,1,512]{2,1,0:T(1,128)S(1)}, u32[]{:S(2)}, u32[]{:S(2)}) collective-permute-start(f32[16,1,512]{2,1,0:T(1,128)S(1)} %get-tuple-element.38), channel_id=1, source_target_pairs={{8,0},{16,8},{24,16},{32,24},{40,32},{48,40},{56,48},{64,56},{72,6... | collective-permute-start | bytes 98312 | tf_op jit(solution)/shard_map/ppermute | solution.py:12
  110.2 8.6 %collective-permute-start.8 = (f32[16,1,512]{2,1,0:T(1,128)S(1)}, f32[16,1,512]{2,1,0:T(1,128)S(1)}, u32[]{:S(2)}, u32[]{:S(2)}) collective-permute-start(f32[16,1,512]{2,1,0:T(1,128)S(1)} %get-tuple-element.39), channel_id=1, source_target_pairs={{0,8},{8,16},{16,24},{24,32},{32,40},{40,48},{48,56},{56,64},{64,7... | collective-permute-start | bytes 98312 | tf_op jit(solution)/shard_map/ppermute | solution.py:12
  (19 other events, 176.7 us)
